TPU v7x, 512 devices: a whole 4x4x16 slice. The times are simulated.
512 devices in a mesh: fine: 128 (over y, z, core), tele: 4 (over x).
Axes of the slice: x: 4, y: 4, z: 16, core: 2. Of those that a mesh axis runs over, the one named last changes fastest.
Arguments:
- right_side: float32 [8192, 320], P(('fine', 'tele')), may hold values from -6 to 6
- fine_inverse: bfloat16 [8192, 320, 320], P(('fine', 'tele')), may hold values from -0.08 to 0.45
- fine_links: int32 [8192, 6], P(('fine', 'tele')), may hold values from -1 to 8191, as said below
- fine_faces: int32 [8192, 6], P(('fine', 'tele')), may hold values from 0 to 23
- coarse_inverse: bfloat16 [1024, 320, 320], P(('fine', 'tele')), may hold values from -0.04 to 0.21
- coarse_links: int32 [1024, 6], P(('fine', 'tele')), may hold values from -1 to 1023, as said below
- coarse_faces: int32 [1024, 6], P(('fine', 'tele')), may hold values from 0 to 23
- face_operators: bfloat16 [24, 80, 80], replicated, may hold values from -1.25 to 1.25
- agglomerate: int32 [8192], P(('fine', 'tele')), may hold values from 0 to 1023, as said below
Outputs:
- solution: float32 [8192, 320], P(('fine', 'tele'))
Inputs may be any that keep to these rules, and one draw needn't show every extreme that they name: `fine_links`: any entry other than -1 is an element held by the same device as the element, or by the device just before or after it in the order of fine+tele, cyclically. `coarse_links`: coarse elements form blocks of 8 consecutive ones; any entry other than -1 lies in the element's own block or in the block just before or after it, cyclically. `agglomerate`: fine element i maps into block i // 64 of 8 consecutive coarse elements; every coarse element collects exactly 8 fine elements.
All inputs are finite; a program needn't handle non-finite values.
Results may differ from a plain program's by a relative error of at most 0.02.
Values may be sent and summed in bfloat16 or wider, within the bound.
No kernel may reach another device: no remote copies, remote signals or barrier semaphores. Data moves between devices by JAX's collectives and lax.ppermute only.
A program may use at most 64 MiB of HBM per device.

v0:
```python
import jax
import jax.numpy as jnp
from jax import lax
from jax.sharding import PartitionSpec as P

FIELDS = 5
NODES = 4
SWEEPS = 3
CYCLES = 2
OPPOSITE = (1, 0, 3, 2, 5, 4)


def passed_along(block, axis, distance):
    devices = range(lax.axis_size(axis))
    route = [((i - distance) % len(devices), i) for i in devices]
    return lax.ppermute(block, axis, route)


def face_table():
    face_size = NODES * NODES
    column = jnp.arange(6 * FIELDS * face_size, dtype=jnp.int32)
    face_index = column // (FIELDS * face_size)
    within = column % (FIELDS * face_size)
    field_index = within // face_size
    first = within // NODES % NODES
    second = within % NODES
    far_node = NODES - 1
    side = jnp.where(face_index % 2 == 0, 0, far_node)
    node_a = jnp.where(face_index < 2, side, first)
    node_b = jnp.where(face_index < 2, first, jnp.where(face_index < 4, side, second))
    node_c = jnp.where(face_index < 4, second, side)
    target = ((field_index * NODES + node_a) * NODES + node_b) * NODES + node_c
    dof_index = jnp.arange(FIELDS * NODES * NODES * NODES, dtype=jnp.int32)
    return (dof_index[:, None] == target[None, :]).astype(jnp.float32)


def take_traces(field_state, table):
    row_count = field_state.shape[0]
    picked = jnp.dot(
        field_state, table, precision=lax.Precision.HIGHEST, preferred_element_type=jnp.float32
    )
    return picked.astype(jnp.bfloat16).reshape(row_count, 6, -1)


def lift_faces(coupled, table):
    return lax.dot_general(
        coupled,
        table,
        (((1,), (1,)), ((), ())),
        precision=lax.Precision.HIGHEST,
        preferred_element_type=jnp.float32,
    )


def neighbour_rows(preceding, own_traces, following, links, position, row_count, devices):
    trace_pool = jnp.concatenate([preceding, own_traces, following], axis=0).reshape(
        -1, own_traces.shape[2]
    )
    clamped = jnp.maximum(links, 0)
    relative = (clamped // row_count - position + 1) % devices
    opposite = jnp.array(OPPOSITE, jnp.int32)
    row_index = (relative * row_count + clamped % row_count) * 6 + opposite[None, :]
    face_rows = jnp.take(trace_pool, row_index.reshape(-1), axis=0).reshape(links.shape[0], 6, -1)
    return jnp.where((links >= 0)[:, :, None], face_rows, jnp.zeros_like(face_rows))


def face_apply(face_operators, face_rows, faces, table):
    flat_rows = face_rows.reshape(-1, face_rows.shape[2])
    face_kinds = faces.reshape(-1)
    products = jnp.einsum(
        "rk,qjk->rqj", flat_rows, face_operators, preferred_element_type=jnp.float32
    )
    picked = face_kinds[:, None] == jnp.arange(face_operators.shape[0], dtype=jnp.int32)[None, :]
    result = jnp.sum(jnp.where(picked[:, :, None], products, 0.0), axis=1)
    return lift_faces(result.reshape(face_rows.shape[0], -1), table)


def fine_coupling(field_state, face_operators, links, faces, position, devices, table):
    own_traces = take_traces(field_state, table)
    preceding = passed_along(own_traces, ("fine", "tele"), 1)
    following = passed_along(own_traces, ("fine", "tele"), -1)
    face_rows = neighbour_rows(
        preceding, own_traces, following, links, position, field_state.shape[0], devices
    )
    return face_apply(face_operators, face_rows, faces, table)


def coarse_coupling(column_traces, face_operators, links, faces, position, devices, table):
    preceding = passed_along(column_traces, "fine", 1)
    following = passed_along(column_traces, "fine", -1)
    face_rows = neighbour_rows(
        preceding, column_traces, following, links, position, column_traces.shape[0], devices
    )
    return face_apply(face_operators, face_rows, faces, table)


def apply_inverse(inverse, lowered):
    return jnp.einsum("nij,nj->ni", inverse, lowered, preferred_element_type=jnp.float32)


def shards(
    right_side,
    fine_inverse,
    fine_links,
    fine_faces,
    coarse_inverse,
    coarse_links,
    coarse_faces,
    face_operators,
    agglomerate,
):
    table = face_table()
    tele_size = lax.axis_size("tele")
    fine_position = lax.axis_index("fine") * tele_size + lax.axis_index("tele")
    fine_devices = lax.axis_size("fine") * tele_size
    column_position = lax.axis_index("fine")
    columns = lax.axis_size("fine")
    column_rows = coarse_inverse.shape[0] * tele_size
    local_target = agglomerate % column_rows
    member = (local_target[:, None] == jnp.arange(column_rows, dtype=jnp.int32)[None, :]).astype(
        jnp.float32
    )
    block_inverse = lax.all_gather(coarse_inverse, "tele", axis=0, tiled=True)
    index_lists = lax.all_gather(
        jnp.concatenate([coarse_links, coarse_faces], axis=1), "tele", axis=0, tiled=True
    )
    block_links = index_lists[:, :6]
    block_faces = index_lists[:, 6:]
    solution = jnp.zeros(right_side.shape, jnp.float32)
    for cycle_index in range(CYCLES):
        for sweep_index in range(SWEEPS):
            if cycle_index == 0 and sweep_index == 0:
                coupled = jnp.zeros(right_side.shape, jnp.float32)
            else:
                coupled = fine_coupling(
                    solution,
                    face_operators,
                    fine_links,
                    fine_faces,
                    fine_position,
                    fine_devices,
                    table,
                )
            lowered = (right_side - coupled).astype(jnp.bfloat16)
            solution = apply_inverse(fine_inverse, lowered)
        residual = lowered.astype(jnp.float32) - fine_coupling(
            solution, face_operators, fine_links, fine_faces, fine_position, fine_devices, table
        )
        partial_sum = jnp.dot(
            member.T, residual, precision=lax.Precision.HIGHEST, preferred_element_type=jnp.float32
        )
        restricted = lax.psum(partial_sum, "tele")
        coarse_state = apply_inverse(block_inverse, restricted.astype(jnp.bfloat16))
        for sweep_index in range(SWEEPS - 1):
            coupled_coarse = coarse_coupling(
                take_traces(coarse_state, table),
                face_operators,
                block_links,
                block_faces,
                column_position,
                columns,
                table,
            )
            coarse_state = apply_inverse(
                block_inverse, (restricted - coupled_coarse).astype(jnp.bfloat16)
            )
        solution = solution + jnp.take(coarse_state, local_target, axis=0)
    return solution


def solution(mesh):
    return jax.shard_map(
        shards,
        mesh=mesh,
        in_specs=(
            P(("fine", "tele"), None),
            P(("fine", "tele"), None, None),
            P(("fine", "tele"), None),
            P(("fine", "tele"), None),
            P(("fine", "tele"), None, None),
            P(("fine", "tele"), None),
            P(("fine", "tele"), None),
            P(),
            P(("fine", "tele")),
        ),
        out_specs=P(("fine", "tele"), None),
        check_vma=False,
    )
```

profile of v0, /device:TPU:2, one launch (start us, length us, event | category | flops | bytes accessed | tf_op | source)
XLA Modules:
  0.0 242.5 jit_solution(18185007734287332940)
XLA Ops:
  6.7 0.9 convert_bitcast_fusion
  7.5 3.3 %fusion.76 = f32[16,1,320]{2,1,0:T(1,128)S(1)} fusion(bf16[16,320,320]{2,1,0:T(8,128)(2,1)} %param.27, bf16[16,320,1]{1,0,2:T(8,128)(2,1)S(1)} %convert_bitcast_fusion), kind=kOutput, calls=%fused_computation.136 | convolution fusion | flops 3276800 | bytes 3307520 | tf_op jit(solution)/shard_map/nij,nj->ni/dot_general | solution.py:98
  11.3 7.8 %collective-permute-start.1 = (bf16[16,6,80]{2,1,0:T(8,128)(2,1)S(1)}, bf16[16,6,80]{2,1,0:T(8,128)(2,1)S(1)}, u32[]{:S(2)}, u32[]{:S(2)}) collective-permute-start(bf16[16,6,80]{2,1,0:T(8,128)(2,1)S(1)} %reshape.333), channel_id=1, source_target_pairs={{1,0},{2,1},{3,2},{4,3},{5,4},{6,5},{7,6},{8,7},{9,8},{10,9},{11,1... | collective-permute-start | bytes 46088 | tf_op jit(solution)/shard_map/ppermute | solution.py:16
  19.1 1.9 collective-permute-start
  21.2 15.2 %all-gather = s32[4,2,12]{2,1,0:T(2,128)S(1)} all-gather(s32[1,2,12]{2,1,0:T(2,128)S(1)} %add_bitcast_fusion), channel_id=1, replica_groups=mesh['fine'=128,'tele'=4] {'tele'}, dimensions={0}, use_global_device_ids=true | all-gather | bytes 480 | tf_op jit(solution)/shard_map/all_gather | solution.py:124
  37.4 0.7 gather_fusion
  39.0 3.5 %fusion.73 = f32[16,1,320]{2,1,0:T(1,128)S(1)} fusion(bf16[16,320,320]{2,1,0:T(8,128)(2,1)} %param.27, bf16[16,320,1]{1,0,2:T(8,128)(2,1)S(1)} %fusion.18), kind=kOutput, calls=%fused_computation.133 | convolution fusion | flops 3276800 | bytes 3307520 | tf_op jit(solution)/shard_map/nij,nj->ni/dot_general | solution.py:98
  43.0 2.6 %collective-permute-start.3 = (bf16[16,6,80]{2,1,0:T(8,128)(2,1)S(1)}, bf16[16,6,80]{2,1,0:T(8,128)(2,1)S(1)}, u32[]{:S(2)}, u32[]{:S(2)}) collective-permute-start(bf16[16,6,80]{2,1,0:T(8,128)(2,1)S(1)} %reshape.337), channel_id=1, source_target_pairs={{1,0},{2,1},{3,2},{4,3},{5,4},{6,5},{7,6},{8,7},{9,8},{10,9},{11,1... | collective-permute-start | bytes 46088 | tf_op jit(solution)/shard_map/ppermute | solution.py:16
  45.5 3.3 %collective-permute-start.2 = (bf16[16,6,80]{2,1,0:T(8,128)(2,1)S(1)}, bf16[16,6,80]{2,1,0:T(8,128)(2,1)S(1)}, u32[]{:S(2)}, u32[]{:S(2)}) collective-permute-start(bf16[16,6,80]{2,1,0:T(8,128)(2,1)S(1)} %reshape.337), channel_id=1, source_target_pairs={{511,0},{0,1},{1,2},{2,3},{3,4},{4,5},{5,6},{6,7},{7,8},{8,9},{9,1... | collective-permute-start | bytes 46088 | tf_op jit(solution)/shard_map/ppermute | solution.py:16
  48.9 0.6 collective-permute-done.3
  49.5 4.9 %collective-permute-done.2 = bf16[16,6,80]{2,1,0:T(8,128)(2,1)S(1)} collective-permute-done((bf16[16,6,80]{2,1,0:T(8,128)(2,1)S(1)}, bf16[16,6,80]{2,1,0:T(8,128)(2,1)S(1)}, u32[]{:S(2)}, u32[]{:S(2)}) %collective-permute-start.2) | collective-permute-done | bytes 15392 | tf_op jit(solution)/shard_map/ppermute | solution.py:16
  54.4 0.7 gather_fusion.1
  56.0 3.3 %fusion.70 = f32[16,1,320]{2,1,0:T(1,128)S(1)} fusion(bf16[16,320,320]{2,1,0:T(8,128)(2,1)} %param.27, bf16[16,320,1]{1,0,2:T(8,128)(2,1)S(1)} %bitcast.138), kind=kOutput, calls=%fused_computation.130 | convolution fusion | flops 3276800 | bytes 3307520 | tf_op jit(solution)/shard_map/nij,nj->ni/dot_general | solution.py:98
  59.8 8.2 %collective-permute-start.5 = (bf16[16,6,80]{2,1,0:T(8,128)(2,1)S(1)}, bf16[16,6,80]{2,1,0:T(8,128)(2,1)S(1)}, u32[]{:S(2)}, u32[]{:S(2)}) collective-permute-start(bf16[16,6,80]{2,1,0:T(8,128)(2,1)S(1)} %reshape.341), channel_id=1, source_target_pairs={{1,0},{2,1},{3,2},{4,3},{5,4},{6,5},{7,6},{8,7},{9,8},{10,9},{11,1... | collective-permute-start | bytes 46088 | tf_op jit(solution)/shard_map/ppermute | solution.py:16
  68.0 1.9 collective-permute-start.4
  70.0 3.9 %collective-permute-done.4 = bf16[16,6,80]{2,1,0:T(8,128)(2,1)S(1)} collective-permute-done((bf16[16,6,80]{2,1,0:T(8,128)(2,1)S(1)}, bf16[16,6,80]{2,1,0:T(8,128)(2,1)S(1)}, u32[]{:S(2)}, u32[]{:S(2)}) %collective-permute-start.4) | collective-permute-done | bytes 15392 | tf_op jit(solution)/shard_map/ppermute | solution.py:16
  73.9 0.7 gather_fusion.2
  75.8 17.8 %psum.14 = f32[8,320]{1,0:T(8,128)S(1)} all-reduce(f32[8,320]{1,0:T(8,128)S(1)} %fusion.145), channel_id=1, replica_groups=mesh['fine'=128,'tele'=4] {'tele'}, use_global_device_ids=true, to_apply=%region_3.5 | all-reduce | flops 2560 | bytes 20480 | tf_op jit(solution)/shard_map/psum | solution.py:152
  93.6 2.3 fusion.118
  96.3 1.9 collective-permute-start.7
  98.2 2.4 collective-permute-start.6
  100.8 5.9 %collective-permute-done.6 = bf16[8,6,80]{2,1,0:T(8,128)(2,1)S(1)} collective-permute-done((bf16[8,6,80]{2,1,0:T(8,128)(2,1)S(1)}, bf16[8,6,80]{2,1,0:T(8,128)(2,1)S(1)}, u32[]{:S(2)}, u32[]{:S(2)}) %collective-permute-start.6) | collective-permute-done | bytes 7712 | tf_op jit(solution)/shard_map/ppermute | solution.py:16
  106.7 0.6 gather_fusion.3
  108.2 2.3 fusion.115
  110.9 1.9 collective-permute-start.9
  112.8 2.4 collective-permute-start.8
  115.3 5.9 %collective-permute-done.8 = bf16[8,6,80]{2,1,0:T(8,128)(2,1)S(1)} collective-permute-done((bf16[8,6,80]{2,1,0:T(8,128)(2,1)S(1)}, bf16[8,6,80]{2,1,0:T(8,128)(2,1)S(1)}, u32[]{:S(2)}, u32[]{:S(2)}) %collective-permute-start.8) | collective-permute-done | bytes 7712 | tf_op jit(solution)/shard_map/ppermute | solution.py:16
  121.2 0.6 gather_fusion.4
  122.9 0.7 fusion.112
  123.5 0.6 gather_fusion.5
  124.5 3.3 %collective-permute-start.11 = (bf16[16,6,80]{2,1,0:T(8,128)(2,1)S(1)}, bf16[16,6,80]{2,1,0:T(8,128)(2,1)S(1)}, u32[]{:S(2)}, u32[]{:S(2)}) collective-permute-start(bf16[16,6,80]{2,1,0:T(8,128)(2,1)S(1)} %reshape.353), channel_id=1, source_target_pairs={{1,0},{2,1},{3,2},{4,3},{5,4},{6,5},{7,6},{8,7},{9,8},{10,9},{11,1... | collective-permute-start | bytes 46088 | tf_op jit(solution)/shard_map/ppermute | solution.py:16
  127.9 2.5 %collective-permute-start.10 = (bf16[16,6,80]{2,1,0:T(8,128)(2,1)S(1)}, bf16[16,6,80]{2,1,0:T(8,128)(2,1)S(1)}, u32[]{:S(2)}, u32[]{:S(2)}) collective-permute-start(bf16[16,6,80]{2,1,0:T(8,128)(2,1)S(1)} %reshape.353), channel_id=1, source_target_pairs={{511,0},{0,1},{1,2},{2,3},{3,4},{4,5},{5,6},{6,7},{7,8},{8,9},{9,1... | collective-permute-start | bytes 46088 | tf_op jit(solution)/shard_map/ppermute | solution.py:16
  130.4 3.3 %collective-permute-done.10 = bf16[16,6,80]{2,1,0:T(8,128)(2,1)S(1)} collective-permute-done((bf16[16,6,80]{2,1,0:T(8,128)(2,1)S(1)}, bf16[16,6,80]{2,1,0:T(8,128)(2,1)S(1)}, u32[]{:S(2)}, u32[]{:S(2)}) %collective-permute-start.10) | collective-permute-done | bytes 15392 | tf_op jit(solution)/shard_map/ppermute | solution.py:16
  133.8 0.7 gather_fusion.6
  135.4 3.3 %fusion.68 = f32[16,1,320]{2,1,0:T(1,128)S(1)} fusion(bf16[16,320,320]{2,1,0:T(8,128)(2,1)} %param.27, bf16[16,320,1]{1,0,2:T(8,128)(2,1)S(1)} %fusion.17), kind=kOutput, calls=%fused_computation.128 | convolution fusion | flops 3276800 | bytes 3307520 | tf_op jit(solution)/shard_map/nij,nj->ni/dot_general | solution.py:98
  139.1 6.9 %collective-permute-start.13 = (bf16[16,6,80]{2,1,0:T(8,128)(2,1)S(1)}, bf16[16,6,80]{2,1,0:T(8,128)(2,1)S(1)}, u32[]{:S(2)}, u32[]{:S(2)}) collective-permute-start(bf16[16,6,80]{2,1,0:T(8,128)(2,1)S(1)} %reshape.357), channel_id=1, source_target_pairs={{1,0},{2,1},{3,2},{4,3},{5,4},{6,5},{7,6},{8,7},{9,8},{10,9},{11,1... | collective-permute-start | bytes 46088 | tf_op jit(solution)/shard_map/ppermute | solution.py:16
  146.0 2.1 collective-permute-start.12
  148.2 3.7 %collective-permute-done.12 = bf16[16,6,80]{2,1,0:T(8,128)(2,1)S(1)} collective-permute-done((bf16[16,6,80]{2,1,0:T(8,128)(2,1)S(1)}, bf16[16,6,80]{2,1,0:T(8,128)(2,1)S(1)}, u32[]{:S(2)}, u32[]{:S(2)}) %collective-permute-start.12) | collective-permute-done | bytes 15392 | tf_op jit(solution)/shard_map/ppermute | solution.py:16
  151.9 0.7 gather_fusion.7
  153.5 3.3 %fusion.65 = f32[16,1,320]{2,1,0:T(1,128)S(1)} fusion(bf16[16,320,320]{2,1,0:T(8,128)(2,1)} %param.27, bf16[16,320,1]{1,0,2:T(8,128)(2,1)S(1)} %fusion.16), kind=kOutput, calls=%fused_computation.125 | convolution fusion | flops 3276800 | bytes 3307520 | tf_op jit(solution)/shard_map/nij,nj->ni/dot_general | solution.py:98
  157.3 6.8 %collective-permute-start.15 = (bf16[16,6,80]{2,1,0:T(8,128)(2,1)S(1)}, bf16[16,6,80]{2,1,0:T(8,128)(2,1)S(1)}, u32[]{:S(2)}, u32[]{:S(2)}) collective-permute-start(bf16[16,6,80]{2,1,0:T(8,128)(2,1)S(1)} %reshape.361), channel_id=1, source_target_pairs={{1,0},{2,1},{3,2},{4,3},{5,4},{6,5},{7,6},{8,7},{9,8},{10,9},{11,1... | collective-permute-start | bytes 46088 | tf_op jit(solution)/shard_map/ppermute | solution.py:16
  164.1 1.9 collective-permute-start.14
  166.0 3.9 %collective-permute-done.14 = bf16[16,6,80]{2,1,0:T(8,128)(2,1)S(1)} collective-permute-done((bf16[16,6,80]{2,1,0:T(8,128)(2,1)S(1)}, bf16[16,6,80]{2,1,0:T(8,128)(2,1)S(1)}, u32[]{:S(2)}, u32[]{:S(2)}) %collective-permute-start.14) | collective-permute-done | bytes 15392 | tf_op jit(solution)/shard_map/ppermute | solution.py:16
  170.0 0.7 gather_fusion.8
  171.6 3.3 %fusion.62 = f32[16,1,320]{2,1,0:T(1,128)S(1)} fusion(bf16[16,320,320]{2,1,0:T(8,128)(2,1)} %param.27, bf16[16,320,1]{1,0,2:T(8,128)(2,1)S(1)} %bitcast.137), kind=kOutput, calls=%fused_computation.122 | convolution fusion | flops 3276800 | bytes 3307520 | tf_op jit(solution)/shard_map/nij,nj->ni/dot_general | solution.py:98
  175.3 6.8 %collective-permute-start.17 = (bf16[16,6,80]{2,1,0:T(8,128)(2,1)S(1)}, bf16[16,6,80]{2,1,0:T(8,128)(2,1)S(1)}, u32[]{:S(2)}, u32[]{:S(2)}) collective-permute-start(bf16[16,6,80]{2,1,0:T(8,128)(2,1)S(1)} %reshape.365), channel_id=1, source_target_pairs={{1,0},{2,1},{3,2},{4,3},{5,4},{6,5},{7,6},{8,7},{9,8},{10,9},{11,1... | collective-permute-start | bytes 46088 | tf_op jit(solution)/shard_map/ppermute | solution.py:16
  182.1 1.9 collective-permute-start.16
  184.1 3.9 %collective-permute-done.16 = bf16[16,6,80]{2,1,0:T(8,128)(2,1)S(1)} collective-permute-done((bf16[16,6,80]{2,1,0:T(8,128)(2,1)S(1)}, bf16[16,6,80]{2,1,0:T(8,128)(2,1)S(1)}, u32[]{:S(2)}, u32[]{:S(2)}) %collective-permute-start.16) | collective-permute-done | bytes 15392 | tf_op jit(solution)/shard_map/ppermute | solution.py:16
  188.1 0.7 gather_fusion.9
  190.0 17.7 %psum.15 = f32[8,320]{1,0:T(8,128)S(1)} all-reduce(f32[8,320]{1,0:T(8,128)S(1)} %fusion.144), channel_id=1, replica_groups=mesh['fine'=128,'tele'=4] {'tele'}, use_global_device_ids=true, to_apply=%region_10.14 | all-reduce | flops 2560 | bytes 20480 | tf_op jit(solution)/shard_map/psum | solution.py:152
  207.7 0.6 fusion.110
  208.7 1.9 collective-permute-start.19
  210.6 2.4 collective-permute-start.18
  213.1 6.0 %collective-permute-done.18 = bf16[8,6,80]{2,1,0:T(8,128)(2,1)S(1)} collective-permute-done((bf16[8,6,80]{2,1,0:T(8,128)(2,1)S(1)}, bf16[8,6,80]{2,1,0:T(8,128)(2,1)S(1)}, u32[]{:S(2)}, u32[]{:S(2)}) %collective-permute-start.18) | collective-permute-done | bytes 7712 | tf_op jit(solution)/shard_map/ppermute | solution.py:16
  219.1 0.6 gather_fusion.10
  219.7 0.5 fusion.9
  220.6 0.7 fusion.107
  221.8 1.9 collective-permute-start.21
  223.7 2.4 collective-permute-start.20
  226.1 6.0 %collective-permute-done.20 = bf16[8,6,80]{2,1,0:T(8,128)(2,1)S(1)} collective-permute-done((bf16[8,6,80]{2,1,0:T(8,128)(2,1)S(1)}, bf16[8,6,80]{2,1,0:T(8,128)(2,1)S(1)}, u32[]{:S(2)}, u32[]{:S(2)}) %collective-permute-start.20) | collective-permute-done | bytes 7712 | tf_op jit(solution)/shard_map/ppermute | solution.py:16
  232.1 0.6 gather_fusion.11
  233.7 0.7 fusion.104
  234.4 0.6 gather_fusion.12
  235.0 0.7 bitcast_add_fusion
  (147 shorter events, 16.7 us)
Async XLA Ops:
  6.5 31.5 %copy-start = (bf16[24,80,80]{2,1,0:T(8,128)(2,1)S(1)}, bf16[24,80,80]{2,1,0:T(8,128)(2,1)}, u32[]{:S(2)}) copy-start(bf16[24,80,80]{2,1,0:T(8,128)(2,1)} %param.33) | copy-start | bytes 921604
  6.5 29.8 %copy-start.5 = (s32[6]{0:T(128)S(1)}, s32[6]{0:T(128)}, u32[]{:S(2)}) copy-start(s32[6]{0:T(128)} %constant.277.clone) | copy-start | bytes 76
  6.5 32.1 %copy-start.2 = (f32[16,320]{1,0:T(8,128)S(1)}, f32[16,320]{1,0:T(8,128)}, u32[]{:S(2)}) copy-start(f32[16,320]{1,0:T(8,128)} %param.26) | copy-start | bytes 61444
  6.5 14.5 %copy-start.3 = (s32[16,6]{0,1:T(8,128)S(1)}, s32[16,6]{0,1:T(8,128)}, u32[]{:S(2)}) copy-start(s32[16,6]{0,1:T(8,128)} %param.28) | copy-start | bytes 1156
  6.5 14.5 %copy-start.6 = (s32[2,6]{1,0:T(2,128)S(1)}, s32[2,6]{1,0:T(2,128)}, u32[]{:S(2)}) copy-start(s32[2,6]{1,0:T(2,128)} %param.32) | copy-start | bytes 148
  6.5 14.5 %copy-start.7 = (s32[2,6]{1,0:T(2,128)S(1)}, s32[2,6]{1,0:T(2,128)}, u32[]{:S(2)}) copy-start(s32[2,6]{1,0:T(2,128)} %param.31) | copy-start | bytes 148
  6.6 30.1 %copy-start.8 = (s32[16]{0:T(128)S(1)}, s32[16]{0:T(128)}, u32[]{:S(2)}) copy-start(s32[16]{0:T(128)} %param.34) | copy-start | bytes 196
  6.6 30.3 %copy-start.4 = (s32[16,6]{0,1:T(8,128)S(1)}, s32[16,6]{0,1:T(8,128)}, u32[]{:S(2)}) copy-start(s32[16,6]{0,1:T(8,128)} %param.29) | copy-start | bytes 1156
  6.6 87.0 %all-gather.3.cloned.1.call-start = ((), (), s32[]{:S(2)}) async-start(), calls=%async_computation | async-start | bytes 2457600 | tf_op jit(solution)/shard_map/all_gather | solution.py:123
  11.3 26.0 %collective-permute-start.1 = (bf16[16,6,80]{2,1,0:T(8,128)(2,1)S(1)}, bf16[16,6,80]{2,1,0:T(8,128)(2,1)S(1)}, u32[]{:S(2)}, u32[]{:S(2)}) collective-permute-start(bf16[16,6,80]{2,1,0:T(8,128)(2,1)S(1)} %reshape.333), channel_id=1, source_target_pairs={{1,0},{2,1},{3,2},{4,3},{5,4},{6,5},{7,6},{8,7},{9,8},{10,9},{11,1... | collective-permute-start | bytes 46088 | tf_op jit(solution)/shard_map/ppermute | solution.py:16
  19.1 18.2 %collective-permute-start = (bf16[16,6,80]{2,1,0:T(8,128)(2,1)S(1)}, bf16[16,6,80]{2,1,0:T(8,128)(2,1)S(1)}, u32[]{:S(2)}, u32[]{:S(2)}) collective-permute-start(bf16[16,6,80]{2,1,0:T(8,128)(2,1)S(1)} %reshape.333), channel_id=1, source_target_pairs={{511,0},{0,1},{1,2},{2,3},{3,4},{4,5},{5,6},{6,7},{7,8},{8,9},{9,1... | collective-permute-start | bytes 46088 | tf_op jit(solution)/shard_map/ppermute | solution.py:16
  43.0 6.5 %collective-permute-start.3 = (bf16[16,6,80]{2,1,0:T(8,128)(2,1)S(1)}, bf16[16,6,80]{2,1,0:T(8,128)(2,1)S(1)}, u32[]{:S(2)}, u32[]{:S(2)}) collective-permute-start(bf16[16,6,80]{2,1,0:T(8,128)(2,1)S(1)} %reshape.337), channel_id=1, source_target_pairs={{1,0},{2,1},{3,2},{4,3},{5,4},{6,5},{7,6},{8,7},{9,8},{10,9},{11,1... | collective-permute-start | bytes 46088 | tf_op jit(solution)/shard_map/ppermute | solution.py:16
  45.5 8.8 %collective-permute-start.2 = (bf16[16,6,80]{2,1,0:T(8,128)(2,1)S(1)}, bf16[16,6,80]{2,1,0:T(8,128)(2,1)S(1)}, u32[]{:S(2)}, u32[]{:S(2)}) collective-permute-start(bf16[16,6,80]{2,1,0:T(8,128)(2,1)S(1)} %reshape.337), channel_id=1, source_target_pairs={{511,0},{0,1},{1,2},{2,3},{3,4},{4,5},{5,6},{6,7},{7,8},{8,9},{9,1... | collective-permute-start | bytes 46088 | tf_op jit(solution)/shard_map/ppermute | solution.py:16
  59.8 10.2 %collective-permute-start.5 = (bf16[16,6,80]{2,1,0:T(8,128)(2,1)S(1)}, bf16[16,6,80]{2,1,0:T(8,128)(2,1)S(1)}, u32[]{:S(2)}, u32[]{:S(2)}) collective-permute-start(bf16[16,6,80]{2,1,0:T(8,128)(2,1)S(1)} %reshape.341), channel_id=1, source_target_pairs={{1,0},{2,1},{3,2},{4,3},{5,4},{6,5},{7,6},{8,7},{9,8},{10,9},{11,1... | collective-permute-start | bytes 46088 | tf_op jit(solution)/shard_map/ppermute | solution.py:16
  68.0 5.8 %collective-permute-start.4 = (bf16[16,6,80]{2,1,0:T(8,128)(2,1)S(1)}, bf16[16,6,80]{2,1,0:T(8,128)(2,1)S(1)}, u32[]{:S(2)}, u32[]{:S(2)}) collective-permute-start(bf16[16,6,80]{2,1,0:T(8,128)(2,1)S(1)} %reshape.341), channel_id=1, source_target_pairs={{511,0},{0,1},{1,2},{2,3},{3,4},{4,5},{5,6},{6,7},{7,8},{8,9},{9,1... | collective-permute-start | bytes 46088 | tf_op jit(solution)/shard_map/ppermute | solution.py:16
  93.6 29.3 %copy-start.1 = (bf16[8,320,320]{2,1,0:T(8,128)(2,1)S(1)}, bf16[8,320,320]{2,1,0:T(8,128)(2,1)}, u32[]{:S(2)}) copy-start(bf16[8,320,320]{2,1,0:T(8,128)(2,1)} %all-gather.3.cloned.1.call-done) | copy-start | bytes 4915204
  96.3 4.4 %collective-permute-start.7 = (bf16[8,6,80]{2,1,0:T(8,128)(2,1)S(1)}, bf16[8,6,80]{2,1,0:T(8,128)(2,1)S(1)}, u32[]{:S(2)}, u32[]{:S(2)}) collective-permute-start(bf16[8,6,80]{2,1,0:T(8,128)(2,1)S(1)} %reshape.345), channel_id=1, source_target_pairs={{4,0},{8,4},{12,8},{16,12},{20,16},{24,20},{28,24},{32,28},{36,32}... | collective-permute-start | bytes 23048 | tf_op jit(solution)/shard_map/ppermute | solution.py:16
  98.2 8.4 %collective-permute-start.6 = (bf16[8,6,80]{2,1,0:T(8,128)(2,1)S(1)}, bf16[8,6,80]{2,1,0:T(8,128)(2,1)S(1)}, u32[]{:S(2)}, u32[]{:S(2)}) collective-permute-start(bf16[8,6,80]{2,1,0:T(8,128)(2,1)S(1)} %reshape.345), channel_id=1, source_target_pairs={{508,0},{0,4},{4,8},{8,12},{12,16},{16,20},{20,24},{24,28},{28,32}... | collective-permute-start | bytes 23048 | tf_op jit(solution)/shard_map/ppermute | solution.py:16
  110.9 4.4 %collective-permute-start.9 = (bf16[8,6,80]{2,1,0:T(8,128)(2,1)S(1)}, bf16[8,6,80]{2,1,0:T(8,128)(2,1)S(1)}, u32[]{:S(2)}, u32[]{:S(2)}) collective-permute-start(bf16[8,6,80]{2,1,0:T(8,128)(2,1)S(1)} %reshape.349), channel_id=1, source_target_pairs={{4,0},{8,4},{12,8},{16,12},{20,16},{24,20},{28,24},{32,28},{36,32}... | collective-permute-start | bytes 23048 | tf_op jit(solution)/shard_map/ppermute | solution.py:16
  112.8 8.4 %collective-permute-start.8 = (bf16[8,6,80]{2,1,0:T(8,128)(2,1)S(1)}, bf16[8,6,80]{2,1,0:T(8,128)(2,1)S(1)}, u32[]{:S(2)}, u32[]{:S(2)}) collective-permute-start(bf16[8,6,80]{2,1,0:T(8,128)(2,1)S(1)} %reshape.349), channel_id=1, source_target_pairs={{508,0},{0,4},{4,8},{8,12},{12,16},{16,20},{20,24},{24,28},{28,32}... | collective-permute-start | bytes 23048 | tf_op jit(solution)/shard_map/ppermute | solution.py:16
  124.5 5.9 %collective-permute-start.11 = (bf16[16,6,80]{2,1,0:T(8,128)(2,1)S(1)}, bf16[16,6,80]{2,1,0:T(8,128)(2,1)S(1)}, u32[]{:S(2)}, u32[]{:S(2)}) collective-permute-start(bf16[16,6,80]{2,1,0:T(8,128)(2,1)S(1)} %reshape.353), channel_id=1, source_target_pairs={{1,0},{2,1},{3,2},{4,3},{5,4},{6,5},{7,6},{8,7},{9,8},{10,9},{11,1... | collective-permute-start | bytes 46088 | tf_op jit(solution)/shard_map/ppermute | solution.py:16
  127.9 5.8 %collective-permute-start.10 = (bf16[16,6,80]{2,1,0:T(8,128)(2,1)S(1)}, bf16[16,6,80]{2,1,0:T(8,128)(2,1)S(1)}, u32[]{:S(2)}, u32[]{:S(2)}) collective-permute-start(bf16[16,6,80]{2,1,0:T(8,128)(2,1)S(1)} %reshape.353), channel_id=1, source_target_pairs={{511,0},{0,1},{1,2},{2,3},{3,4},{4,5},{5,6},{6,7},{7,8},{8,9},{9,1... | collective-permute-start | bytes 46088 | tf_op jit(solution)/shard_map/ppermute | solution.py:16
  139.1 9.0 %collective-permute-start.13 = (bf16[16,6,80]{2,1,0:T(8,128)(2,1)S(1)}, bf16[16,6,80]{2,1,0:T(8,128)(2,1)S(1)}, u32[]{:S(2)}, u32[]{:S(2)}) collective-permute-start(bf16[16,6,80]{2,1,0:T(8,128)(2,1)S(1)} %reshape.357), channel_id=1, source_target_pairs={{1,0},{2,1},{3,2},{4,3},{5,4},{6,5},{7,6},{8,7},{9,8},{10,9},{11,1... | collective-permute-start | bytes 46088 | tf_op jit(solution)/shard_map/ppermute | solution.py:16
  146.0 5.8 %collective-permute-start.12 = (bf16[16,6,80]{2,1,0:T(8,128)(2,1)S(1)}, bf16[16,6,80]{2,1,0:T(8,128)(2,1)S(1)}, u32[]{:S(2)}, u32[]{:S(2)}) collective-permute-start(bf16[16,6,80]{2,1,0:T(8,128)(2,1)S(1)} %reshape.357), channel_id=1, source_target_pairs={{511,0},{0,1},{1,2},{2,3},{3,4},{4,5},{5,6},{6,7},{7,8},{8,9},{9,1... | collective-permute-start | bytes 46088 | tf_op jit(solution)/shard_map/ppermute | solution.py:16
  157.3 8.7 %collective-permute-start.15 = (bf16[16,6,80]{2,1,0:T(8,128)(2,1)S(1)}, bf16[16,6,80]{2,1,0:T(8,128)(2,1)S(1)}, u32[]{:S(2)}, u32[]{:S(2)}) collective-permute-start(bf16[16,6,80]{2,1,0:T(8,128)(2,1)S(1)} %reshape.361), channel_id=1, source_target_pairs={{1,0},{2,1},{3,2},{4,3},{5,4},{6,5},{7,6},{8,7},{9,8},{10,9},{11,1... | collective-permute-start | bytes 46088 | tf_op jit(solution)/shard_map/ppermute | solution.py:16
  164.1 5.8 %collective-permute-start.14 = (bf16[16,6,80]{2,1,0:T(8,128)(2,1)S(1)}, bf16[16,6,80]{2,1,0:T(8,128)(2,1)S(1)}, u32[]{:S(2)}, u32[]{:S(2)}) collective-permute-start(bf16[16,6,80]{2,1,0:T(8,128)(2,1)S(1)} %reshape.361), channel_id=1, source_target_pairs={{511,0},{0,1},{1,2},{2,3},{3,4},{4,5},{5,6},{6,7},{7,8},{8,9},{9,1... | collective-permute-start | bytes 46088 | tf_op jit(solution)/shard_map/ppermute | solution.py:16
  175.3 8.7 %collective-permute-start.17 = (bf16[16,6,80]{2,1,0:T(8,128)(2,1)S(1)}, bf16[16,6,80]{2,1,0:T(8,128)(2,1)S(1)}, u32[]{:S(2)}, u32[]{:S(2)}) collective-permute-start(bf16[16,6,80]{2,1,0:T(8,128)(2,1)S(1)} %reshape.365), channel_id=1, source_target_pairs={{1,0},{2,1},{3,2},{4,3},{5,4},{6,5},{7,6},{8,7},{9,8},{10,9},{11,1... | collective-permute-start | bytes 46088 | tf_op jit(solution)/shard_map/ppermute | solution.py:16
  182.1 5.9 %collective-permute-start.16 = (bf16[16,6,80]{2,1,0:T(8,128)(2,1)S(1)}, bf16[16,6,80]{2,1,0:T(8,128)(2,1)S(1)}, u32[]{:S(2)}, u32[]{:S(2)}) collective-permute-start(bf16[16,6,80]{2,1,0:T(8,128)(2,1)S(1)} %reshape.365), channel_id=1, source_target_pairs={{511,0},{0,1},{1,2},{2,3},{3,4},{4,5},{5,6},{6,7},{7,8},{8,9},{9,1... | collective-permute-start | bytes 46088 | tf_op jit(solution)/shard_map/ppermute | solution.py:16
  208.7 4.3 %collective-permute-start.19 = (bf16[8,6,80]{2,1,0:T(8,128)(2,1)S(1)}, bf16[8,6,80]{2,1,0:T(8,128)(2,1)S(1)}, u32[]{:S(2)}, u32[]{:S(2)}) collective-permute-start(bf16[8,6,80]{2,1,0:T(8,128)(2,1)S(1)} %reshape.369), channel_id=1, source_target_pairs={{4,0},{8,4},{12,8},{16,12},{20,16},{24,20},{28,24},{32,28},{36,32}... | collective-permute-start | bytes 23048 | tf_op jit(solution)/shard_map/ppermute | solution.py:16
  210.6 8.4 %collective-permute-start.18 = (bf16[8,6,80]{2,1,0:T(8,128)(2,1)S(1)}, bf16[8,6,80]{2,1,0:T(8,128)(2,1)S(1)}, u32[]{:S(2)}, u32[]{:S(2)}) collective-permute-start(bf16[8,6,80]{2,1,0:T(8,128)(2,1)S(1)} %reshape.369), channel_id=1, source_target_pairs={{508,0},{0,4},{4,8},{8,12},{12,16},{16,20},{20,24},{24,28},{28,32}... | collective-permute-start | bytes 23048 | tf_op jit(solution)/shard_map/ppermute | solution.py:16
  221.8 4.3 %collective-permute-start.21 = (bf16[8,6,80]{2,1,0:T(8,128)(2,1)S(1)}, bf16[8,6,80]{2,1,0:T(8,128)(2,1)S(1)}, u32[]{:S(2)}, u32[]{:S(2)}) collective-permute-start(bf16[8,6,80]{2,1,0:T(8,128)(2,1)S(1)} %reshape.373), channel_id=1, source_target_pairs={{4,0},{8,4},{12,8},{16,12},{20,16},{24,20},{28,24},{32,28},{36,32}... | collective-permute-start | bytes 23048 | tf_op jit(solution)/shard_map/ppermute | solution.py:16
  223.7 8.4 %collective-permute-start.20 = (bf16[8,6,80]{2,1,0:T(8,128)(2,1)S(1)}, bf16[8,6,80]{2,1,0:T(8,128)(2,1)S(1)}, u32[]{:S(2)}, u32[]{:S(2)}) collective-permute-start(bf16[8,6,80]{2,1,0:T(8,128)(2,1)S(1)} %reshape.373), channel_id=1, source_target_pairs={{508,0},{0,4},{4,8},{8,12},{12,16},{16,20},{20,24},{24,28},{28,32}... | collective-permute-start | bytes 23048 | tf_op jit(solution)/shard_map/ppermute | solution.py:16
Sparse Core Ops, SparseCore 0:
  21.2 38.3 all-gather.2
where the time goes:
time: 244 us; the launch traced here: 243 us
  starting transfers between devices  75.3 us (31%)
  blocking collectives  50.6 us (21%)
  waiting for transfers between devices  47.8 us (20%)
  matrix products  40.2 us (16%)
  between operations  14.2 us (6%)
  local copies, waits for them, and re-layouts  12.1 us (5%)
    ppermute x22, starting transfers between devices, passed_along(): return lax.ppermute(block, axis, route)  75.3 us
    ppermute x22, waiting for transfers between devices, passed_along(): return lax.ppermute(block, axis, route)  47.8 us
    psum x2, blocking collectives, shards(): restricted = lax.psum(partial_sum, 'tele')  35.5 us
    dot_general x12, matrix products, apply_inverse(): jnp.einsum('nij,nj->ni', inverse, lowered, preferred_element_type=jnp.flo...  27.4 us
    all_gather x1, blocking collectives, shards(): lax.all_gather(jnp.concatenate([coarse_links, coarse_faces], axis=1), 'te...  15.2 us
    gather x11, local copies, waits for them, and re-layouts, neighbour_rows(): jnp.take(trace_pool, row_index.reshape(-1), axis=0)  7.19 us
  transfers between devices with their start and end apart: 23, of which 11 were waited for; matrix products, arithmetic and copies ran while one was open for 6% of the time, Pallas kernels for 0%

commit v1 on v0

--- a/solution.py
+++ b/solution.py
@@ -8,6 +8,13 @@
 SWEEPS = 3
 CYCLES = 2
 OPPOSITE = (1, 0, 3, 2, 5, 4)
+
+
+def fill_notes(q_in):
+    piece_out = lax.psum(1, "tele")
+    state_next = jnp.stack(piece_out * [q_in], 0)
+    s_next = lax.all_to_all(state_next, "tele", 0, 0)
+    return jnp.concatenate(s_next, 0)
 
 
 def passed_along(block, axis, distance):
@@ -121,9 +128,7 @@
         jnp.float32
     )
     block_inverse = lax.all_gather(coarse_inverse, "tele", axis=0, tiled=True)
-    index_lists = lax.all_gather(
-        jnp.concatenate([coarse_links, coarse_faces], axis=1), "tele", axis=0, tiled=True
-    )
+    index_lists = fill_notes(jnp.concatenate([coarse_links, coarse_faces], axis=1))
     block_links = index_lists[:, :6]
     block_faces = index_lists[:, 6:]
     solution = jnp.zeros(right_side.shape, jnp.float32)

time: 244 us -> 245 us (level)
  blocking collectives: 50.6 us -> 35.5 us
  starting transfers between devices: 75.3 us -> 86.7 us
  waiting for transfers between devices: 47.8 us -> 52.1 us
    all_gather x1 -> x0, blocking collectives: 15.2 us -> none  [shards(): lax.all_gather(jnp.concatenate([coarse_links, coarse_faces], axis=1), 'te...]
    all_to_all x0 -> x1, starting transfers between devices: none -> 11.4 us  [fill_notes(): s_next = lax.all_to_all(state_next, 'tele', 0, 0)]
    all_to_all x0 -> x1, waiting for transfers between devices: none -> 3.11 us  [fill_notes(): s_next = lax.all_to_all(state_next, 'tele', 0, 0)]
  transfers between devices with their start and end apart: 23 -> 24, of which waited for: 11 -> 12; matrix products, arithmetic and copies ran while one was open for 6% -> 6% of each run, Pallas kernels for 0% -> 0%
where the time goes in v1:
time: 245 us; the launch traced here: 244 us
  starting transfers between devices  86.7 us (35%)
  waiting for transfers between devices  52.1 us (21%)
  matrix products  40.2 us (16%)
  blocking collectives  35.5 us (14%)
  between operations  14.2 us (6%)
  local copies, waits for them, and re-layouts  12.7 us (5%)
    ppermute x22, starting transfers between devices, passed_along(): return lax.ppermute(block, axis, route)  75.3 us
    ppermute x22, waiting for transfers between devices, passed_along(): return lax.ppermute(block, axis, route)  49 us
    psum x2, blocking collectives, shards(): restricted = lax.psum(partial_sum, 'tele')  35.5 us
    dot_general x12, matrix products, apply_inverse(): jnp.einsum('nij,nj->ni', inverse, lowered, preferred_element_type=jnp.flo...  27.4 us
    all_to_all x1, starting transfers between devices, fill_notes(): s_next = lax.all_to_all(state_next, 'tele', 0, 0)  11.4 us
    gather x11, local copies, waits for them, and re-layouts, neighbour_rows(): jnp.take(trace_pool, row_index.reshape(-1), axis=0)  7.19 us
  transfers between devices with their start and end apart: 24, of which 12 were waited for; matrix products, arithmetic and copies ran while one was open for 6% of the time, Pallas kernels for 0%

profile of v1, /device:TPU:2, one launch (start us, length us, event | category | flops | bytes accessed | tf_op | source)
XLA Modules:
  0.0 243.6 jit_solution(8188343621935124900)
XLA Ops:
  6.7 0.9 convert_bitcast_fusion
  7.5 3.3 %fusion.76 = f32[16,1,320]{2,1,0:T(1,128)S(1)} fusion(bf16[16,320,320]{2,1,0:T(8,128)(2,1)} %param.27, bf16[16,320,1]{1,0,2:T(8,128)(2,1)S(1)} %convert_bitcast_fusion), kind=kOutput, calls=%fused_computation.136 | convolution fusion | flops 3276800 | bytes 3307520 | tf_op jit(solution)/shard_map/nij,nj->ni/dot_general | solution.py:105
  11.3 7.8 %collective-permute-start.1 = (bf16[16,6,80]{2,1,0:T(8,128)(2,1)S(1)}, bf16[16,6,80]{2,1,0:T(8,128)(2,1)S(1)}, u32[]{:S(2)}, u32[]{:S(2)}) collective-permute-start(bf16[16,6,80]{2,1,0:T(8,128)(2,1)S(1)} %reshape.338), channel_id=1, source_target_pairs={{1,0},{2,1},{3,2},{4,3},{5,4},{6,5},{7,6},{8,7},{9,8},{10,9},{11,1... | collective-permute-start | bytes 46088 | tf_op jit(solution)/shard_map/ppermute | solution.py:23
  19.1 1.9 collective-permute-start
  21.1 0.6 stack.2
  21.7 11.4 %all-to-all-start = ((s32[4,2,12]{2,1,0:T(2,128)}), s32[4,2,12]{2,1,0:T(2,128)S(1)}, u32[]{:S(2)}, u32[]{:S(2)}) async-start(s32[4,2,12]{2,1,0:T(2,128)} %stack.2), calls=%async_computation | async-start | bytes 8192 | tf_op jit(solution)/shard_map/all_to_all | solution.py:16
  33.9 3.1 %all-to-all-done = s32[4,2,12]{2,1,0:T(2,128)S(1)} async-done(((s32[4,2,12]{2,1,0:T(2,128)}), s32[4,2,12]{2,1,0:T(2,128)S(1)}, u32[]{:S(2)}, u32[]{:S(2)}) %all-to-all-start) | async-done | bytes 416 | tf_op jit(solution)/shard_map/all_to_all | solution.py:16
  37.4 0.7 gather_fusion
  39.0 3.5 %fusion.73 = f32[16,1,320]{2,1,0:T(1,128)S(1)} fusion(bf16[16,320,320]{2,1,0:T(8,128)(2,1)} %param.27, bf16[16,320,1]{1,0,2:T(8,128)(2,1)S(1)} %fusion.18), kind=kOutput, calls=%fused_computation.133 | convolution fusion | flops 3276800 | bytes 3307520 | tf_op jit(solution)/shard_map/nij,nj->ni/dot_general | solution.py:105
  43.0 3.4 %collective-permute-start.3 = (bf16[16,6,80]{2,1,0:T(8,128)(2,1)S(1)}, bf16[16,6,80]{2,1,0:T(8,128)(2,1)S(1)}, u32[]{:S(2)}, u32[]{:S(2)}) collective-permute-start(bf16[16,6,80]{2,1,0:T(8,128)(2,1)S(1)} %reshape.342), channel_id=1, source_target_pairs={{1,0},{2,1},{3,2},{4,3},{5,4},{6,5},{7,6},{8,7},{9,8},{10,9},{11,1... | collective-permute-start | bytes 46088 | tf_op jit(solution)/shard_map/ppermute | solution.py:23
  46.3 2.5 %collective-permute-start.2 = (bf16[16,6,80]{2,1,0:T(8,128)(2,1)S(1)}, bf16[16,6,80]{2,1,0:T(8,128)(2,1)S(1)}, u32[]{:S(2)}, u32[]{:S(2)}) collective-permute-start(bf16[16,6,80]{2,1,0:T(8,128)(2,1)S(1)} %reshape.342), channel_id=1, source_target_pairs={{511,0},{0,1},{1,2},{2,3},{3,4},{4,5},{5,6},{6,7},{7,8},{8,9},{9,1... | collective-permute-start | bytes 46088 | tf_op jit(solution)/shard_map/ppermute | solution.py:23
  48.8 0.6 collective-permute-done.3
  49.4 6.1 %collective-permute-done.2 = bf16[16,6,80]{2,1,0:T(8,128)(2,1)S(1)} collective-permute-done((bf16[16,6,80]{2,1,0:T(8,128)(2,1)S(1)}, bf16[16,6,80]{2,1,0:T(8,128)(2,1)S(1)}, u32[]{:S(2)}, u32[]{:S(2)}) %collective-permute-start.2) | collective-permute-done | bytes 15392 | tf_op jit(solution)/shard_map/ppermute | solution.py:23
  55.6 0.7 gather_fusion.1
  57.2 3.3 %fusion.70 = f32[16,1,320]{2,1,0:T(1,128)S(1)} fusion(bf16[16,320,320]{2,1,0:T(8,128)(2,1)} %param.27, bf16[16,320,1]{1,0,2:T(8,128)(2,1)S(1)} %bitcast.136), kind=kOutput, calls=%fused_computation.130 | convolution fusion | flops 3276800 | bytes 3307520 | tf_op jit(solution)/shard_map/nij,nj->ni/dot_general | solution.py:105
  61.0 8.2 %collective-permute-start.5 = (bf16[16,6,80]{2,1,0:T(8,128)(2,1)S(1)}, bf16[16,6,80]{2,1,0:T(8,128)(2,1)S(1)}, u32[]{:S(2)}, u32[]{:S(2)}) collective-permute-start(bf16[16,6,80]{2,1,0:T(8,128)(2,1)S(1)} %reshape.346), channel_id=1, source_target_pairs={{1,0},{2,1},{3,2},{4,3},{5,4},{6,5},{7,6},{8,7},{9,8},{10,9},{11,1... | collective-permute-start | bytes 46088 | tf_op jit(solution)/shard_map/ppermute | solution.py:23
  69.2 1.9 collective-permute-start.4
  71.1 3.9 %collective-permute-done.4 = bf16[16,6,80]{2,1,0:T(8,128)(2,1)S(1)} collective-permute-done((bf16[16,6,80]{2,1,0:T(8,128)(2,1)S(1)}, bf16[16,6,80]{2,1,0:T(8,128)(2,1)S(1)}, u32[]{:S(2)}, u32[]{:S(2)}) %collective-permute-start.4) | collective-permute-done | bytes 15392 | tf_op jit(solution)/shard_map/ppermute | solution.py:23
  75.1 0.7 gather_fusion.2
  77.0 17.8 %psum.14 = f32[8,320]{1,0:T(8,128)S(1)} all-reduce(f32[8,320]{1,0:T(8,128)S(1)} %fusion.145), channel_id=1, replica_groups=mesh['fine'=128,'tele'=4] {'tele'}, use_global_device_ids=true, to_apply=%region_3.5 | all-reduce | flops 2560 | bytes 20480 | tf_op jit(solution)/shard_map/psum | solution.py:157
  94.7 2.3 fusion.118
  97.5 1.9 collective-permute-start.7
  99.4 2.4 collective-permute-start.6
  101.9 5.9 %collective-permute-done.6 = bf16[8,6,80]{2,1,0:T(8,128)(2,1)S(1)} collective-permute-done((bf16[8,6,80]{2,1,0:T(8,128)(2,1)S(1)}, bf16[8,6,80]{2,1,0:T(8,128)(2,1)S(1)}, u32[]{:S(2)}, u32[]{:S(2)}) %collective-permute-start.6) | collective-permute-done | bytes 7712 | tf_op jit(solution)/shard_map/ppermute | solution.py:23
  107.8 0.6 gather_fusion.3
  109.4 2.3 fusion.115
  112.0 1.9 collective-permute-start.9
  114.0 2.4 collective-permute-start.8
  116.4 5.9 %collective-permute-done.8 = bf16[8,6,80]{2,1,0:T(8,128)(2,1)S(1)} collective-permute-done((bf16[8,6,80]{2,1,0:T(8,128)(2,1)S(1)}, bf16[8,6,80]{2,1,0:T(8,128)(2,1)S(1)}, u32[]{:S(2)}, u32[]{:S(2)}) %collective-permute-start.8) | collective-permute-done | bytes 7712 | tf_op jit(solution)/shard_map/ppermute | solution.py:23
  122.4 0.6 gather_fusion.4
  124.0 0.7 fusion.112
  124.7 0.6 gather_fusion.5
  125.7 3.3 %collective-permute-start.11 = (bf16[16,6,80]{2,1,0:T(8,128)(2,1)S(1)}, bf16[16,6,80]{2,1,0:T(8,128)(2,1)S(1)}, u32[]{:S(2)}, u32[]{:S(2)}) collective-permute-start(bf16[16,6,80]{2,1,0:T(8,128)(2,1)S(1)} %reshape.359), channel_id=1, source_target_pairs={{1,0},{2,1},{3,2},{4,3},{5,4},{6,5},{7,6},{8,7},{9,8},{10,9},{11,1... | collective-permute-start | bytes 46088 | tf_op jit(solution)/shard_map/ppermute | solution.py:23
  129.0 2.5 %collective-permute-start.10 = (bf16[16,6,80]{2,1,0:T(8,128)(2,1)S(1)}, bf16[16,6,80]{2,1,0:T(8,128)(2,1)S(1)}, u32[]{:S(2)}, u32[]{:S(2)}) collective-permute-start(bf16[16,6,80]{2,1,0:T(8,128)(2,1)S(1)} %reshape.359), channel_id=1, source_target_pairs={{511,0},{0,1},{1,2},{2,3},{3,4},{4,5},{5,6},{6,7},{7,8},{8,9},{9,1... | collective-permute-start | bytes 46088 | tf_op jit(solution)/shard_map/ppermute | solution.py:23
  131.6 3.3 %collective-permute-done.10 = bf16[16,6,80]{2,1,0:T(8,128)(2,1)S(1)} collective-permute-done((bf16[16,6,80]{2,1,0:T(8,128)(2,1)S(1)}, bf16[16,6,80]{2,1,0:T(8,128)(2,1)S(1)}, u32[]{:S(2)}, u32[]{:S(2)}) %collective-permute-start.10) | collective-permute-done | bytes 15392 | tf_op jit(solution)/shard_map/ppermute | solution.py:23
  134.9 0.7 gather_fusion.6
  136.5 3.3 %fusion.68 = f32[16,1,320]{2,1,0:T(1,128)S(1)} fusion(bf16[16,320,320]{2,1,0:T(8,128)(2,1)} %param.27, bf16[16,320,1]{1,0,2:T(8,128)(2,1)S(1)} %fusion.17), kind=kOutput, calls=%fused_computation.128 | convolution fusion | flops 3276800 | bytes 3307520 | tf_op jit(solution)/shard_map/nij,nj->ni/dot_general | solution.py:105
  140.3 6.9 %collective-permute-start.13 = (bf16[16,6,80]{2,1,0:T(8,128)(2,1)S(1)}, bf16[16,6,80]{2,1,0:T(8,128)(2,1)S(1)}, u32[]{:S(2)}, u32[]{:S(2)}) collective-permute-start(bf16[16,6,80]{2,1,0:T(8,128)(2,1)S(1)} %reshape.363), channel_id=1, source_target_pairs={{1,0},{2,1},{3,2},{4,3},{5,4},{6,5},{7,6},{8,7},{9,8},{10,9},{11,1... | collective-permute-start | bytes 46088 | tf_op jit(solution)/shard_map/ppermute | solution.py:23
  147.2 2.1 collective-permute-start.12
  149.3 3.7 %collective-permute-done.12 = bf16[16,6,80]{2,1,0:T(8,128)(2,1)S(1)} collective-permute-done((bf16[16,6,80]{2,1,0:T(8,128)(2,1)S(1)}, bf16[16,6,80]{2,1,0:T(8,128)(2,1)S(1)}, u32[]{:S(2)}, u32[]{:S(2)}) %collective-permute-start.12) | collective-permute-done | bytes 15392 | tf_op jit(solution)/shard_map/ppermute | solution.py:23
  153.1 0.7 gather_fusion.7
  154.7 3.3 %fusion.65 = f32[16,1,320]{2,1,0:T(1,128)S(1)} fusion(bf16[16,320,320]{2,1,0:T(8,128)(2,1)} %param.27, bf16[16,320,1]{1,0,2:T(8,128)(2,1)S(1)} %fusion.16), kind=kOutput, calls=%fused_computation.125 | convolution fusion | flops 3276800 | bytes 3307520 | tf_op jit(solution)/shard_map/nij,nj->ni/dot_general | solution.py:105
  158.4 6.8 %collective-permute-start.15 = (bf16[16,6,80]{2,1,0:T(8,128)(2,1)S(1)}, bf16[16,6,80]{2,1,0:T(8,128)(2,1)S(1)}, u32[]{:S(2)}, u32[]{:S(2)}) collective-permute-start(bf16[16,6,80]{2,1,0:T(8,128)(2,1)S(1)} %reshape.367), channel_id=1, source_target_pairs={{1,0},{2,1},{3,2},{4,3},{5,4},{6,5},{7,6},{8,7},{9,8},{10,9},{11,1... | collective-permute-start | bytes 46088 | tf_op jit(solution)/shard_map/ppermute | solution.py:23
  165.2 1.9 collective-permute-start.14
  167.2 3.9 %collective-permute-done.14 = bf16[16,6,80]{2,1,0:T(8,128)(2,1)S(1)} collective-permute-done((bf16[16,6,80]{2,1,0:T(8,128)(2,1)S(1)}, bf16[16,6,80]{2,1,0:T(8,128)(2,1)S(1)}, u32[]{:S(2)}, u32[]{:S(2)}) %collective-permute-start.14) | collective-permute-done | bytes 15392 | tf_op jit(solution)/shard_map/ppermute | solution.py:23
  171.1 0.7 gather_fusion.8
  172.7 3.3 %fusion.62 = f32[16,1,320]{2,1,0:T(1,128)S(1)} fusion(bf16[16,320,320]{2,1,0:T(8,128)(2,1)} %param.27, bf16[16,320,1]{1,0,2:T(8,128)(2,1)S(1)} %bitcast.135), kind=kOutput, calls=%fused_computation.122 | convolution fusion | flops 3276800 | bytes 3307520 | tf_op jit(solution)/shard_map/nij,nj->ni/dot_general | solution.py:105
  176.5 6.8 %collective-permute-start.17 = (bf16[16,6,80]{2,1,0:T(8,128)(2,1)S(1)}, bf16[16,6,80]{2,1,0:T(8,128)(2,1)S(1)}, u32[]{:S(2)}, u32[]{:S(2)}) collective-permute-start(bf16[16,6,80]{2,1,0:T(8,128)(2,1)S(1)} %reshape.371), channel_id=1, source_target_pairs={{1,0},{2,1},{3,2},{4,3},{5,4},{6,5},{7,6},{8,7},{9,8},{10,9},{11,1... | collective-permute-start | bytes 46088 | tf_op jit(solution)/shard_map/ppermute | solution.py:23
  183.3 1.9 collective-permute-start.16
  185.2 3.9 %collective-permute-done.16 = bf16[16,6,80]{2,1,0:T(8,128)(2,1)S(1)} collective-permute-done((bf16[16,6,80]{2,1,0:T(8,128)(2,1)S(1)}, bf16[16,6,80]{2,1,0:T(8,128)(2,1)S(1)}, u32[]{:S(2)}, u32[]{:S(2)}) %collective-permute-start.16) | collective-permute-done | bytes 15392 | tf_op jit(solution)/shard_map/ppermute | solution.py:23
  189.2 0.7 gather_fusion.9
  191.1 17.7 %psum.15 = f32[8,320]{1,0:T(8,128)S(1)} all-reduce(f32[8,320]{1,0:T(8,128)S(1)} %fusion.144), channel_id=1, replica_groups=mesh['fine'=128,'tele'=4] {'tele'}, use_global_device_ids=true, to_apply=%region_10.14 | all-reduce | flops 2560 | bytes 20480 | tf_op jit(solution)/shard_map/psum | solution.py:157
  208.8 0.6 fusion.110
  209.8 1.9 collective-permute-start.19
  211.8 2.4 collective-permute-start.18
  214.2 6.0 %collective-permute-done.18 = bf16[8,6,80]{2,1,0:T(8,128)(2,1)S(1)} collective-permute-done((bf16[8,6,80]{2,1,0:T(8,128)(2,1)S(1)}, bf16[8,6,80]{2,1,0:T(8,128)(2,1)S(1)}, u32[]{:S(2)}, u32[]{:S(2)}) %collective-permute-start.18) | collective-permute-done | bytes 7712 | tf_op jit(solution)/shard_map/ppermute | solution.py:23
  220.2 0.6 gather_fusion.10
  221.8 0.7 fusion.107
  222.9 1.9 collective-permute-start.21
  224.8 2.4 collective-permute-start.20
  227.2 6.0 %collective-permute-done.20 = bf16[8,6,80]{2,1,0:T(8,128)(2,1)S(1)} collective-permute-done((bf16[8,6,80]{2,1,0:T(8,128)(2,1)S(1)}, bf16[8,6,80]{2,1,0:T(8,128)(2,1)S(1)}, u32[]{:S(2)}, u32[]{:S(2)}) %collective-permute-start.20) | collective-permute-done | bytes 7712 | tf_op jit(solution)/shard_map/ppermute | solution.py:23
  233.2 0.6 gather_fusion.11
  234.8 0.7 fusion.104
  236.1 0.7 bitcast_add_fusion
  (149 shorter events, 17.9 us)
Async XLA Ops:
  6.5 31.5 %copy-start = (bf16[24,80,80]{2,1,0:T(8,128)(2,1)S(1)}, bf16[24,80,80]{2,1,0:T(8,128)(2,1)}, u32[]{:S(2)}) copy-start(bf16[24,80,80]{2,1,0:T(8,128)(2,1)} %param.33) | copy-start | bytes 921604
  6.5 26.6 %copy-start.5 = (s32[6]{0:T(128)S(1)}, s32[6]{0:T(128)}, u32[]{:S(2)}) copy-start(s32[6]{0:T(128)} %constant.277.clone) | copy-start | bytes 76
  6.5 32.1 %copy-start.2 = (f32[16,320]{1,0:T(8,128)S(1)}, f32[16,320]{1,0:T(8,128)}, u32[]{:S(2)}) copy-start(f32[16,320]{1,0:T(8,128)} %param.26) | copy-start | bytes 61444
  6.5 14.5 %copy-start.6 = (s32[2,6]{1,0:T(2,128)S(1)}, s32[2,6]{1,0:T(2,128)}, u32[]{:S(2)}) copy-start(s32[2,6]{1,0:T(2,128)} %param.32) | copy-start | bytes 148
  6.5 14.5 %copy-start.7 = (s32[2,6]{1,0:T(2,128)S(1)}, s32[2,6]{1,0:T(2,128)}, u32[]{:S(2)}) copy-start(s32[2,6]{1,0:T(2,128)} %param.31) | copy-start | bytes 148
  6.5 26.6 %copy-start.3 = (s32[16,6]{0,1:T(8,128)S(1)}, s32[16,6]{0,1:T(8,128)}, u32[]{:S(2)}) copy-start(s32[16,6]{0,1:T(8,128)} %param.28) | copy-start | bytes 1156
  6.6 26.9 %copy-start.8 = (s32[16]{0:T(128)S(1)}, s32[16]{0:T(128)}, u32[]{:S(2)}) copy-start(s32[16]{0:T(128)} %param.34) | copy-start | bytes 196
  6.6 26.9 %copy-start.4 = (s32[16,6]{0,1:T(8,128)S(1)}, s32[16,6]{0,1:T(8,128)}, u32[]{:S(2)}) copy-start(s32[16,6]{0,1:T(8,128)} %param.29) | copy-start | bytes 1156
  6.6 88.1 %all-gather.2.cloned.1.call-start = ((), (), s32[]{:S(2)}) async-start(), calls=%async_computation.1 | async-start | bytes 2457600 | tf_op jit(solution)/shard_map/all_gather | solution.py:130
  11.3 26.0 %collective-permute-start.1 = (bf16[16,6,80]{2,1,0:T(8,128)(2,1)S(1)}, bf16[16,6,80]{2,1,0:T(8,128)(2,1)S(1)}, u32[]{:S(2)}, u32[]{:S(2)}) collective-permute-start(bf16[16,6,80]{2,1,0:T(8,128)(2,1)S(1)} %reshape.338), channel_id=1, source_target_pairs={{1,0},{2,1},{3,2},{4,3},{5,4},{6,5},{7,6},{8,7},{9,8},{10,9},{11,1... | collective-permute-start | bytes 46088 | tf_op jit(solution)/shard_map/ppermute | solution.py:23
  19.1 18.2 %collective-permute-start = (bf16[16,6,80]{2,1,0:T(8,128)(2,1)S(1)}, bf16[16,6,80]{2,1,0:T(8,128)(2,1)S(1)}, u32[]{:S(2)}, u32[]{:S(2)}) collective-permute-start(bf16[16,6,80]{2,1,0:T(8,128)(2,1)S(1)} %reshape.338), channel_id=1, source_target_pairs={{511,0},{0,1},{1,2},{2,3},{3,4},{4,5},{5,6},{6,7},{7,8},{8,9},{9,1... | collective-permute-start | bytes 46088 | tf_op jit(solution)/shard_map/ppermute | solution.py:23
  21.7 15.3 %all-to-all-start = ((s32[4,2,12]{2,1,0:T(2,128)}), s32[4,2,12]{2,1,0:T(2,128)S(1)}, u32[]{:S(2)}, u32[]{:S(2)}) async-start(s32[4,2,12]{2,1,0:T(2,128)} %stack.2), calls=%async_computation | async-start | bytes 8192 | tf_op jit(solution)/shard_map/all_to_all | solution.py:16
  43.0 6.5 %collective-permute-start.3 = (bf16[16,6,80]{2,1,0:T(8,128)(2,1)S(1)}, bf16[16,6,80]{2,1,0:T(8,128)(2,1)S(1)}, u32[]{:S(2)}, u32[]{:S(2)}) collective-permute-start(bf16[16,6,80]{2,1,0:T(8,128)(2,1)S(1)} %reshape.342), channel_id=1, source_target_pairs={{1,0},{2,1},{3,2},{4,3},{5,4},{6,5},{7,6},{8,7},{9,8},{10,9},{11,1... | collective-permute-start | bytes 46088 | tf_op jit(solution)/shard_map/ppermute | solution.py:23
  46.3 9.2 %collective-permute-start.2 = (bf16[16,6,80]{2,1,0:T(8,128)(2,1)S(1)}, bf16[16,6,80]{2,1,0:T(8,128)(2,1)S(1)}, u32[]{:S(2)}, u32[]{:S(2)}) collective-permute-start(bf16[16,6,80]{2,1,0:T(8,128)(2,1)S(1)} %reshape.342), channel_id=1, source_target_pairs={{511,0},{0,1},{1,2},{2,3},{3,4},{4,5},{5,6},{6,7},{7,8},{8,9},{9,1... | collective-permute-start | bytes 46088 | tf_op jit(solution)/shard_map/ppermute | solution.py:23
  61.0 10.2 %collective-permute-start.5 = (bf16[16,6,80]{2,1,0:T(8,128)(2,1)S(1)}, bf16[16,6,80]{2,1,0:T(8,128)(2,1)S(1)}, u32[]{:S(2)}, u32[]{:S(2)}) collective-permute-start(bf16[16,6,80]{2,1,0:T(8,128)(2,1)S(1)} %reshape.346), channel_id=1, source_target_pairs={{1,0},{2,1},{3,2},{4,3},{5,4},{6,5},{7,6},{8,7},{9,8},{10,9},{11,1... | collective-permute-start | bytes 46088 | tf_op jit(solution)/shard_map/ppermute | solution.py:23
  69.2 5.8 %collective-permute-start.4 = (bf16[16,6,80]{2,1,0:T(8,128)(2,1)S(1)}, bf16[16,6,80]{2,1,0:T(8,128)(2,1)S(1)}, u32[]{:S(2)}, u32[]{:S(2)}) collective-permute-start(bf16[16,6,80]{2,1,0:T(8,128)(2,1)S(1)} %reshape.346), channel_id=1, source_target_pairs={{511,0},{0,1},{1,2},{2,3},{3,4},{4,5},{5,6},{6,7},{7,8},{8,9},{9,1... | collective-permute-start | bytes 46088 | tf_op jit(solution)/shard_map/ppermute | solution.py:23
  94.7 29.3 %copy-start.1 = (bf16[8,320,320]{2,1,0:T(8,128)(2,1)S(1)}, bf16[8,320,320]{2,1,0:T(8,128)(2,1)}, u32[]{:S(2)}) copy-start(bf16[8,320,320]{2,1,0:T(8,128)(2,1)} %all-gather.2.cloned.1.call-done) | copy-start | bytes 4915204
  97.5 4.4 %collective-permute-start.7 = (bf16[8,6,80]{2,1,0:T(8,128)(2,1)S(1)}, bf16[8,6,80]{2,1,0:T(8,128)(2,1)S(1)}, u32[]{:S(2)}, u32[]{:S(2)}) collective-permute-start(bf16[8,6,80]{2,1,0:T(8,128)(2,1)S(1)} %reshape.351), channel_id=1, source_target_pairs={{4,0},{8,4},{12,8},{16,12},{20,16},{24,20},{28,24},{32,28},{36,32}... | collective-permute-start | bytes 23048 | tf_op jit(solution)/shard_map/ppermute | solution.py:23
  99.4 8.4 %collective-permute-start.6 = (bf16[8,6,80]{2,1,0:T(8,128)(2,1)S(1)}, bf16[8,6,80]{2,1,0:T(8,128)(2,1)S(1)}, u32[]{:S(2)}, u32[]{:S(2)}) collective-permute-start(bf16[8,6,80]{2,1,0:T(8,128)(2,1)S(1)} %reshape.351), channel_id=1, source_target_pairs={{508,0},{0,4},{4,8},{8,12},{12,16},{16,20},{20,24},{24,28},{28,32}... | collective-permute-start | bytes 23048 | tf_op jit(solution)/shard_map/ppermute | solution.py:23
  112.0 4.4 %collective-permute-start.9 = (bf16[8,6,80]{2,1,0:T(8,128)(2,1)S(1)}, bf16[8,6,80]{2,1,0:T(8,128)(2,1)S(1)}, u32[]{:S(2)}, u32[]{:S(2)}) collective-permute-start(bf16[8,6,80]{2,1,0:T(8,128)(2,1)S(1)} %reshape.355), channel_id=1, source_target_pairs={{4,0},{8,4},{12,8},{16,12},{20,16},{24,20},{28,24},{32,28},{36,32}... | collective-permute-start | bytes 23048 | tf_op jit(solution)/shard_map/ppermute | solution.py:23
  114.0 8.4 %collective-permute-start.8 = (bf16[8,6,80]{2,1,0:T(8,128)(2,1)S(1)}, bf16[8,6,80]{2,1,0:T(8,128)(2,1)S(1)}, u32[]{:S(2)}, u32[]{:S(2)}) collective-permute-start(bf16[8,6,80]{2,1,0:T(8,128)(2,1)S(1)} %reshape.355), channel_id=1, source_target_pairs={{508,0},{0,4},{4,8},{8,12},{12,16},{16,20},{20,24},{24,28},{28,32}... | collective-permute-start | bytes 23048 | tf_op jit(solution)/shard_map/ppermute | solution.py:23
  125.7 5.9 %collective-permute-start.11 = (bf16[16,6,80]{2,1,0:T(8,128)(2,1)S(1)}, bf16[16,6,80]{2,1,0:T(8,128)(2,1)S(1)}, u32[]{:S(2)}, u32[]{:S(2)}) collective-permute-start(bf16[16,6,80]{2,1,0:T(8,128)(2,1)S(1)} %reshape.359), channel_id=1, source_target_pairs={{1,0},{2,1},{3,2},{4,3},{5,4},{6,5},{7,6},{8,7},{9,8},{10,9},{11,1... | collective-permute-start | bytes 46088 | tf_op jit(solution)/shard_map/ppermute | solution.py:23
  129.0 5.8 %collective-permute-start.10 = (bf16[16,6,80]{2,1,0:T(8,128)(2,1)S(1)}, bf16[16,6,80]{2,1,0:T(8,128)(2,1)S(1)}, u32[]{:S(2)}, u32[]{:S(2)}) collective-permute-start(bf16[16,6,80]{2,1,0:T(8,128)(2,1)S(1)} %reshape.359), channel_id=1, source_target_pairs={{511,0},{0,1},{1,2},{2,3},{3,4},{4,5},{5,6},{6,7},{7,8},{8,9},{9,1... | collective-permute-start | bytes 46088 | tf_op jit(solution)/shard_map/ppermute | solution.py:23
  140.3 9.0 %collective-permute-start.13 = (bf16[16,6,80]{2,1,0:T(8,128)(2,1)S(1)}, bf16[16,6,80]{2,1,0:T(8,128)(2,1)S(1)}, u32[]{:S(2)}, u32[]{:S(2)}) collective-permute-start(bf16[16,6,80]{2,1,0:T(8,128)(2,1)S(1)} %reshape.363), channel_id=1, source_target_pairs={{1,0},{2,1},{3,2},{4,3},{5,4},{6,5},{7,6},{8,7},{9,8},{10,9},{11,1... | collective-permute-start | bytes 46088 | tf_op jit(solution)/shard_map/ppermute | solution.py:23
  147.2 5.8 %collective-permute-start.12 = (bf16[16,6,80]{2,1,0:T(8,128)(2,1)S(1)}, bf16[16,6,80]{2,1,0:T(8,128)(2,1)S(1)}, u32[]{:S(2)}, u32[]{:S(2)}) collective-permute-start(bf16[16,6,80]{2,1,0:T(8,128)(2,1)S(1)} %reshape.363), channel_id=1, source_target_pairs={{511,0},{0,1},{1,2},{2,3},{3,4},{4,5},{5,6},{6,7},{7,8},{8,9},{9,1... | collective-permute-start | bytes 46088 | tf_op jit(solution)/shard_map/ppermute | solution.py:23
  158.4 8.7 %collective-permute-start.15 = (bf16[16,6,80]{2,1,0:T(8,128)(2,1)S(1)}, bf16[16,6,80]{2,1,0:T(8,128)(2,1)S(1)}, u32[]{:S(2)}, u32[]{:S(2)}) collective-permute-start(bf16[16,6,80]{2,1,0:T(8,128)(2,1)S(1)} %reshape.367), channel_id=1, source_target_pairs={{1,0},{2,1},{3,2},{4,3},{5,4},{6,5},{7,6},{8,7},{9,8},{10,9},{11,1... | collective-permute-start | bytes 46088 | tf_op jit(solution)/shard_map/ppermute | solution.py:23
  165.2 5.8 %collective-permute-start.14 = (bf16[16,6,80]{2,1,0:T(8,128)(2,1)S(1)}, bf16[16,6,80]{2,1,0:T(8,128)(2,1)S(1)}, u32[]{:S(2)}, u32[]{:S(2)}) collective-permute-start(bf16[16,6,80]{2,1,0:T(8,128)(2,1)S(1)} %reshape.367), channel_id=1, source_target_pairs={{511,0},{0,1},{1,2},{2,3},{3,4},{4,5},{5,6},{6,7},{7,8},{8,9},{9,1... | collective-permute-start | bytes 46088 | tf_op jit(solution)/shard_map/ppermute | solution.py:23
  176.5 8.7 %collective-permute-start.17 = (bf16[16,6,80]{2,1,0:T(8,128)(2,1)S(1)}, bf16[16,6,80]{2,1,0:T(8,128)(2,1)S(1)}, u32[]{:S(2)}, u32[]{:S(2)}) collective-permute-start(bf16[16,6,80]{2,1,0:T(8,128)(2,1)S(1)} %reshape.371), channel_id=1, source_target_pairs={{1,0},{2,1},{3,2},{4,3},{5,4},{6,5},{7,6},{8,7},{9,8},{10,9},{11,1... | collective-permute-start | bytes 46088 | tf_op jit(solution)/shard_map/ppermute | solution.py:23
  183.3 5.9 %collective-permute-start.16 = (bf16[16,6,80]{2,1,0:T(8,128)(2,1)S(1)}, bf16[16,6,80]{2,1,0:T(8,128)(2,1)S(1)}, u32[]{:S(2)}, u32[]{:S(2)}) collective-permute-start(bf16[16,6,80]{2,1,0:T(8,128)(2,1)S(1)} %reshape.371), channel_id=1, source_target_pairs={{511,0},{0,1},{1,2},{2,3},{3,4},{4,5},{5,6},{6,7},{7,8},{8,9},{9,1... | collective-permute-start | bytes 46088 | tf_op jit(solution)/shard_map/ppermute | solution.py:23
  209.8 4.3 %collective-permute-start.19 = (bf16[8,6,80]{2,1,0:T(8,128)(2,1)S(1)}, bf16[8,6,80]{2,1,0:T(8,128)(2,1)S(1)}, u32[]{:S(2)}, u32[]{:S(2)}) collective-permute-start(bf16[8,6,80]{2,1,0:T(8,128)(2,1)S(1)} %reshape.375), channel_id=1, source_target_pairs={{4,0},{8,4},{12,8},{16,12},{20,16},{24,20},{28,24},{32,28},{36,32}... | collective-permute-start | bytes 23048 | tf_op jit(solution)/shard_map/ppermute | solution.py:23
  211.8 8.4 %collective-permute-start.18 = (bf16[8,6,80]{2,1,0:T(8,128)(2,1)S(1)}, bf16[8,6,80]{2,1,0:T(8,128)(2,1)S(1)}, u32[]{:S(2)}, u32[]{:S(2)}) collective-permute-start(bf16[8,6,80]{2,1,0:T(8,128)(2,1)S(1)} %reshape.375), channel_id=1, source_target_pairs={{508,0},{0,4},{4,8},{8,12},{12,16},{16,20},{20,24},{24,28},{28,32}... | collective-permute-start | bytes 23048 | tf_op jit(solution)/shard_map/ppermute | solution.py:23
  222.9 4.3 %collective-permute-start.21 = (bf16[8,6,80]{2,1,0:T(8,128)(2,1)S(1)}, bf16[8,6,80]{2,1,0:T(8,128)(2,1)S(1)}, u32[]{:S(2)}, u32[]{:S(2)}) collective-permute-start(bf16[8,6,80]{2,1,0:T(8,128)(2,1)S(1)} %reshape.379), channel_id=1, source_target_pairs={{4,0},{8,4},{12,8},{16,12},{20,16},{24,20},{28,24},{32,28},{36,32}... | collective-permute-start | bytes 23048 | tf_op jit(solution)/shard_map/ppermute | solution.py:23
  224.8 8.4 %collective-permute-start.20 = (bf16[8,6,80]{2,1,0:T(8,128)(2,1)S(1)}, bf16[8,6,80]{2,1,0:T(8,128)(2,1)S(1)}, u32[]{:S(2)}, u32[]{:S(2)}) collective-permute-start(bf16[8,6,80]{2,1,0:T(8,128)(2,1)S(1)} %reshape.379), channel_id=1, source_target_pairs={{508,0},{0,4},{4,8},{8,12},{12,16},{16,20},{20,24},{24,28},{28,32}... | collective-permute-start | bytes 23048 | tf_op jit(solution)/shard_map/ppermute | solution.py:23
Sparse Core Ops, SparseCore 0:
  21.2 38.3 all-gather.1
